TPU v7x, 128 devices: a whole 4x4x4 slice. The times are simulated.
128 devices in a mesh: grp: 8 (over x_hi, y), mem: 16 (over x_lo, z, core).
Axes of the slice: x: 4 (x_hi: 2, x_lo: 2; x = x_hi * 2 + x_lo), y: 4, z: 4, core: 2. Of those that a mesh axis runs over, the one named last changes fastest.
Arguments:
- activations: bfloat16 [4096, 32, 4096], P(('grp', 'mem')), may hold values from -6 to 6
- out_grads: bfloat16 [4096, 32, 4096], P(('grp', 'mem')), may hold values from -6 to 6
- proj_in: bfloat16 [4096, 64], replicated, may hold values from -1 to 1
- proj_out: bfloat16 [4096, 64], replicated, may hold values from -1 to 1
- basis_in: float32 [64, 64], replicated, may hold values from -1 to 1
- basis_out: float32 [64, 64], replicated, may hold values from -1 to 1
- eigen: float32 [64, 64], replicated, may hold values from 0.05 to 12
- doc_ids: int32 [4096], P(('grp', 'mem')), may hold values from 0 to 1023
Outputs:
- scores: float32 [4096, 4096], P(('grp', 'mem'))
All inputs are finite; a program needn't handle non-finite values.
Results may differ from a plain program's by a relative error of at most 0.0077.
Values may be sent and summed in bfloat16 or wider, within the bound.
A program may use at most 192 MiB of HBM per device.

v0:
```python
import jax
import jax.numpy as jnp
from jax import lax
from jax.sharding import PartitionSpec as P

damping = 0.1


def score_block(own_feat, own_ids, other_feat, other_ids, factor):
    products = lax.dot_general(
        own_feat, other_feat, (((1,), (1,)), ((), ())), preferred_element_type=jnp.float32
    )
    products = products * factor
    same_doc = own_ids[:, None] == other_ids[None, :]
    return jnp.where(same_doc, jnp.float32(0.0), products)


def on_device(activations, out_grads, proj_in, proj_out, basis_in, basis_out, eigen, doc_ids):
    high = lax.Precision.HIGHEST
    local_count, tokens, width = activations.shape
    rank = proj_in.shape[1]
    factor = 1.0 / (tokens * rank)
    act_proj = jnp.dot(
        activations.reshape(-1, width), proj_in, preferred_element_type=jnp.float32
    ).astype(jnp.bfloat16)
    grad_proj = jnp.dot(
        out_grads.reshape(-1, width), proj_out, preferred_element_type=jnp.float32
    ).astype(jnp.bfloat16)
    act_proj = act_proj.reshape(local_count, tokens, rank)
    grad_proj = grad_proj.reshape(local_count, tokens, rank)
    grad_feat = jnp.einsum("etr,ets->ers", grad_proj, act_proj, preferred_element_type=jnp.float32)
    rotated = jnp.einsum("ers,ru->eus", grad_feat, basis_out, precision=high)
    rotated = jnp.einsum("eus,sv->euv", rotated, basis_in, precision=high)
    scaled = (
        (rotated / jnp.sqrt(eigen + damping)).astype(jnp.bfloat16).reshape(local_count, rank * rank)
    )
    return score_block(
        scaled,
        doc_ids,
        lax.all_gather(scaled, ("grp", "mem"), axis=0, tiled=True),
        lax.all_gather(doc_ids, ("grp", "mem"), axis=0, tiled=True),
        factor,
    )


def solution(mesh):
    return jax.shard_map(
        on_device,
        mesh=mesh,
        in_specs=(
            P(("grp", "mem"), None, None),
            P(("grp", "mem"), None, None),
            P(),
            P(),
            P(),
            P(),
            P(),
            P(("grp", "mem")),
        ),
        out_specs=P(("grp", "mem"), None),
        check_vma=False,
    )
```

profile of v0, /device:TPU:1, one launch (start us, length us, event | category | flops | bytes accessed | tf_op | source)
XLA Modules:
  0.0 283.6 jit_solution(6873357665614955712)
XLA Ops:
  6.5 0.0 copy-start
  6.5 0.0 all-gather.2.cloned.1.call-start
  6.5 0.9 add_sqrt_fusion
  7.4 0.2 copy-done
  7.6 6.0 %convolution_convert_fusion = bf16[1024,64]{0,1:T(8,128)(2,1)S(1)} fusion(bf16[1024,4096]{1,0:T(8,128)(2,1)} %bitcast.22, bf16[4096,64]{0,1:T(8,128)(2,1)S(1)} %copy-done), kind=kOutput, calls=%fused_computation.5 | convolution fusion | flops 536936448 | bytes 9043968 | tf_op jit(solution)/shard_map/dot_general | solution.py:23
  13.6 0.0 copy-start.2
  13.6 0.0 copy-start.4
  13.6 0.2 copy.10
  13.8 0.0 copy-done.1
  13.8 0.0 copy-start.3
  13.8 6.0 %convolution_convert_fusion.1 = bf16[1024,64]{0,1:T(8,128)(2,1)S(1)} fusion(bf16[1024,4096]{1,0:T(8,128)(2,1)} %bitcast.23, bf16[4096,64]{0,1:T(8,128)(2,1)S(1)} %copy-done.1), kind=kOutput, calls=%fused_computation.6 | convolution fusion | flops 536936448 | bytes 9043968 | tf_op jit(solution)/shard_map/dot_general | solution.py:26
  19.9 0.2 copy.9
  20.1 0.3 fusion.4
  20.4 0.0 copy-done.2
  20.4 1.0 convolution_bitcast_fusion
  21.5 0.0 copy-done.4
  21.5 1.0 fusion.1
  22.5 1.2 reshape.22
  23.6 0.0 all-gather.2.cloned.1.call-update
  23.7 0.0 copy-done.3
  23.7 0.3 dynamic-update-slice
  24.0 68.7 %all-reduce = s32[4096]{0:T(1024)S(1)} all-reduce(s32[4096]{0:T(1024)S(1)} %dynamic-update-slice), channel_id=1, replica_groups=mesh['grp'=8,'mem'=16] {'grp','mem'}, use_global_device_ids=true, to_apply=%add | all-reduce | flops 4096 | bytes 32768
  92.6 168.1 %all-gather.2.cloned.1.call-done = bf16[4096,4096]{1,0:T(8,128)(2,1)} async-done(((bf16[32,4096]{1,0:T(8,128)(2,1)}), bf16[4096,4096]{1,0:T(8,128)(2,1)}) %all-gather.2.cloned.1.call-update) | async-done | bytes 33554448 | tf_op jit(solution)/shard_map/all_gather | solution.py:40
  260.7 16.0 %fusion = f32[32,4096]{1,0:T(8,128)} fusion(bf16[32,4096]{1,0:T(8,128)(2,1)} %reshape.22, bf16[4096,4096]{1,0:T(8,128)(2,1)} %all-gather.2.cloned.1.call-done, s32[4096]{0:T(1024)S(1)} %all-reduce, s32[32]{0:T(128)S(1)} %copy-done.3), kind=kOutput, calls=%fused_computation.1 | convolution fusion | flops 1074135040 | bytes 34357376 | tf_op jit(solution)/shard_map/dot_general | solution.py:10
  (2 shorter events, 0.0 us)
Async XLA Ops:
  6.5 1.1 copy-start
  6.5 7.3 %copy-start.1 = (bf16[4096,64]{0,1:T(8,128)(2,1)S(1)}, bf16[4096,64]{0,1:T(8,128)(2,1)}, u32[]{:S(2)}) copy-start(bf16[4096,64]{0,1:T(8,128)(2,1)} %param.11) | copy-start | bytes 1572868
  6.5 254.2 %all-gather.2.cloned.1.call-start = ((), (), s32[]{:S(2)}) async-start(), calls=%async_computation | async-start | bytes 33816576 | tf_op jit(solution)/shard_map/all_gather | solution.py:40
  13.6 6.8 %copy-start.2 = (f32[64,64]{1,0:T(8,128)S(1)}, f32[64,64]{1,0:T(8,128)}, u32[]{:S(2)}) copy-start(f32[64,64]{1,0:T(8,128)} %param.13) | copy-start | bytes 49156
  13.6 7.8 %copy-start.4 = (f32[64,64]{1,0:T(8,128)S(1)}, f32[64,64]{1,0:T(8,128)}, u32[]{:S(2)}) copy-start(f32[64,64]{1,0:T(8,128)} %param.12) | copy-start | bytes 49156
  13.8 9.8 %copy-start.3 = (s32[32]{0:T(128)S(1)}, s32[32]{0:T(128)}, u32[]{:S(2)}) copy-start(s32[32]{0:T(128)} %param.15) | copy-start | bytes 388
Sparse Core Ops, SparseCore 0:
  23.8 236.9 all-gather.1
where the time goes:
time: 284 us
  waiting for transfers between devices  168 us (59%)
  blocking collectives  68.7 us (24%)
  matrix products  30.5 us (11%)
  between operations  13.5 us (5%)
    all_gather x1, waiting for transfers between devices, on_device(): lax.all_gather(scaled, ('grp', 'mem'), axis=0, tiled=True)  168 us
    unnamed x1, blocking collectives  68.7 us
    dot_general x1, matrix products, score_block(): lax.dot_general(own_feat, other_feat, (((1,), (1,)), ((), ())), preferred...  16 us
    dot_general x1, matrix products, on_device(): jnp.dot(out_grads.reshape(-1, width), proj_out, preferred_element_type=jn...  6.04 us
    dot_general x1, matrix products, on_device(): jnp.dot(activations.reshape(-1, width), proj_in, preferred_element_type=j...  6.03 us
  transfers between devices with their start and end apart: 1, of which 1 were waited for; matrix products, arithmetic and copies ran while one was open for 0% of the time, Pallas kernels for 0%

commit v1 on v0

v1 whole, which is shorter than its diff:
```python
import functools

import jax
import jax.numpy as jnp
from jax import lax
from jax.experimental import pallas as pl
from jax.experimental.pallas import tpu as pltpu
from jax.sharding import PartitionSpec as P

damping = 0.1
BF = jnp.bfloat16
F32 = jnp.float32
MESH = pl.DeviceIdType.MESH
NT = (((1,), (1,)), ((), ()))


def dot(a, b):
    return jnp.dot(a, b, preferred_element_type=F32)


def split(value):
    high = value.astype(BF)
    return high, (value - high.astype(F32)).astype(BF)


def feature_kernel(
    act_hbm, grad_hbm, pin_hbm, pout_hbm, bin_ref, bout_ref, eig_ref, out_ref,
    act, grad, w_in, w_out, w_g, scale, dsem, wsem,
):
    copies = []
    for part in range(4):
        rows = pl.ds(part * 256, 256)
        copies.append(
            (
                pltpu.make_async_copy(act_hbm.at[rows], act.at[rows], dsem.at[part]),
                pltpu.make_async_copy(grad_hbm.at[rows], grad.at[rows], dsem.at[4 + part]),
            )
        )
    weights = (
        pltpu.make_async_copy(pin_hbm, w_in.at[pl.ds(0, 64)], wsem.at[0]),
        pltpu.make_async_copy(pout_hbm, w_out.at[pl.ds(64, 64)], wsem.at[1]),
    )
    for copy in weights:
        copy.start()
    for pair in copies:
        for copy in pair:
            copy.start()
    w_in[64:, :] = jnp.zeros((64, 4096), BF)
    w_out[:64, :] = jnp.zeros((64, 4096), BF)

    zeros = jnp.zeros((64, 64), BF)
    out_high, out_low = split(bout_ref[...])
    stacked = jnp.concatenate([zeros, out_high, zeros, out_low], axis=0)
    for tile in range(16):
        unit = lax.broadcasted_iota(jnp.int32, (64, 256), 0)
        lane = lax.broadcasted_iota(jnp.int32, (64, 256), 1)
        spread = jnp.where(lax.div(lane, 64) + tile * 4 == unit, 1.0, 0.0).astype(BF)
        w_g[:, tile * 256 : (tile + 1) * 256] = dot(stacked, spread).astype(BF)
    in_high, in_low = split(bin_ref[...])
    wide_zeros = jnp.zeros((64, 128), BF)
    w_a = jnp.concatenate(
        [
            jnp.concatenate([in_high, in_high], axis=1),
            wide_zeros,
            jnp.concatenate([in_low, in_low], axis=1),
            wide_zeros,
        ],
        axis=0,
    )
    inverse = 1.0 / jnp.sqrt(eig_ref[...] + damping)
    for tile in range(32):
        scale[:, tile * 128 : (tile + 1) * 128] = jnp.concatenate(
            [inverse[2 * tile : 2 * tile + 1], inverse[2 * tile + 1 : 2 * tile + 2]], axis=1
        )
    row = lax.broadcasted_iota(jnp.int32, (256, 256), 0)
    col = lax.broadcasted_iota(jnp.int32, (256, 256), 1)
    perm = jnp.where(lax.rem(row, 8) * 32 + lax.div(row, 8) == col, 1.0, 0.0).astype(BF)

    for copy in weights:
        copy.wait()
    for half in range(2):
        both, twice = [], []
        for sub in range(2):
            part = half * 2 + sub
            for copy in copies[part]:
                copy.wait()
            rows = pl.ds(part * 256, 256)
            projected = lax.dot_general(
                act[rows, :], w_in[...], NT, preferred_element_type=F32
            ) + lax.dot_general(grad[rows, :], w_out[...], NT, preferred_element_type=F32)
            moved = dot(perm, projected.astype(BF)).astype(BF)
            pair = jnp.concatenate([moved, moved], axis=1)
            rotated = dot(pair, w_a)
            both.append(pair)
            twice.append(jnp.concatenate([rotated, rotated], axis=1))
        for tile in range(16):
            lanes = slice(tile * 256, (tile + 1) * 256)
            sums = []
            for sub in range(2):
                product = dot(both[sub], w_g[:, lanes]) * twice[sub]
                sums.append(jnp.sum(product.reshape(32, 8, 256), axis=0))
            out_ref[half, :, lanes] = (
                jnp.concatenate(sums, axis=0) * scale[:, lanes]
            ).astype(BF)


def features(act, grad, pin, pout, basis_in, basis_out, eigen):
    vmem = pl.BlockSpec(memory_space=pltpu.VMEM)
    hbm = pl.BlockSpec(memory_space=pl.ANY)
    return pl.pallas_call(
        feature_kernel,
        out_shape=jax.ShapeDtypeStruct((2, 16, 4096), BF),
        in_specs=[hbm] * 4 + [vmem] * 3,
        out_specs=vmem,
        scratch_shapes=[
            pltpu.VMEM((1024, 4096), BF),
            pltpu.VMEM((1024, 4096), BF),
            pltpu.VMEM((128, 4096), BF),
            pltpu.VMEM((128, 4096), BF),
            pltpu.VMEM((256, 4096), BF),
            pltpu.VMEM((1, 4096), F32),
            pltpu.SemaphoreType.DMA((8,)),
            pltpu.SemaphoreType.DMA((2,)),
        ],
        compiler_params=pltpu.CompilerParams(vmem_limit_bytes=60 << 20),
        name="features",
    )(act, grad, pin, pout, basis_in, basis_out, eigen)


def score_kernel(
    feat_hbm, ids_ref, out_ref,
    rowbuf, colbuf, res_send, res_recv, id_col, id_row, row_ids, col_ids,
    lsem, ssem, rsem, isend, irecv, osend, orecv,
    *, factor,
):
    g = lax.axis_index("grp")
    m = lax.axis_index("mem")
    x = lax.div(g, 4) * 2 + lax.div(m, 8)
    y = lax.rem(g, 4)
    z = lax.rem(lax.div(m, 2), 4)
    c = lax.rem(m, 2)
    odd = lax.rem(z, 2)
    zr = lax.rem(z + 3 + 2 * odd, 4)
    zc = z + 1 - 2 * odd
    xm, xp, x2 = lax.rem(x + 3, 4), lax.rem(x + 1, 4), lax.rem(x + 2, 4)
    ym, yp, y2 = lax.rem(y + 3, 4), lax.rem(y + 1, 4), lax.rem(y + 2, 4)
    oc = 1 - c

    def device(x, y, z, c):
        return (lax.div(x, 2) * 4 + y, lax.rem(x, 2) * 8 + z * 2 + c)

    def slot(y, z, c):
        return y * 4 + lax.rem(z, 2) * 2 + c

    row_places = [(a, b) for b in (z, zr) for a in (x, xm, xp, x2)]
    row_peers = [device(a, y, b, c) for a, b in row_places[1:]]
    col_places = [(a, b) for b in (z, zc) for a in (y, ym, yp, y2)]
    col_peers = [device(x, a, b, c) for a, b in col_places[1:]]
    cross_peers = [device(x, a, b, oc) for a, b in col_places]

    local = [
        pltpu.make_async_copy(feat_hbm, rowbuf.at[0], lsem.at[0]),
        pltpu.make_async_copy(feat_hbm, colbuf.at[slot(y, z, c)], lsem.at[1]),
    ]
    for copy in local:
        copy.start()
    barrier = pltpu.get_barrier_semaphore()
    everyone = row_peers + col_peers + cross_peers
    for peer in everyone:
        pl.semaphore_signal(barrier, inc=1, device_id=peer, device_id_type=MESH)

    lane = lax.broadcasted_iota(jnp.int32, (8, 128), 1)
    first = (odd * 2 + c) * 32
    placed = jnp.zeros((8, 128), jnp.int32)
    for example in range(32):
        value = ids_ref[example]
        placed = jnp.where(lane == first + example, value, placed)
        id_col[example : example + 1, :] = jnp.full((1, 128), value, jnp.int32)
    id_row[...] = placed
    row_ids[0] = id_col[...]
    col_ids[slot(y, z, c)] = placed

    for copy in local:
        copy.wait()
    pl.semaphore_wait(barrier, len(everyone))

    started = []

    def send(src, dst, send_sem, recv_sem, peer):
        copy = pltpu.make_async_remote_copy(
            src_ref=src, dst_ref=dst, send_sem=send_sem, recv_sem=recv_sem,
            device_id=peer, device_id_type=MESH,
        )
        copy.start()
        started.append(copy)

    own = slot(y, z, c)
    to = {
        "x+": device(xp, y, z, c), "x-": device(xm, y, z, c),
        "y+": device(x, yp, z, c), "y-": device(x, ym, z, c),
        "zr": device(x, y, zr, c), "zc": device(x, y, zc, c),
        "core": device(x, y, z, oc),
    }
    count = [0]

    def piece(src, dst, number, where):
        send(src, dst, ssem.at[count[0]], rsem.at[number], to[where])
        count[0] += 1

    def row(k, half):
        return rowbuf.at[k, half]

    def col(index, half):
        return colbuf.at[index, half]

    def row_number(k, half):
        return (k - 1) * 2 + half

    col_names = ["own", "ym", "yp", "y2", "zc", "zcym", "zcyp", "zcy2"]

    def col_number(name, half):
        return 14 + (col_names.index(name) - 1) * 2 + half

    def cross_number(name, half):
        return 28 + col_names.index(name) * 2 + half

    slots = {name: slot(a, b, c) for name, (a, b) in zip(col_names, col_places)}
    other = {name: slot(a, b, oc) for name, (a, b) in zip(col_names, col_places)}

    def row_wait(k, half):
        ref = row(k, half)
        pltpu.make_async_copy(ref, ref, rsem.at[row_number(k, half)]).wait()

    def col_wait(name, half):
        ref = col(slots[name], half)
        pltpu.make_async_copy(ref, ref, rsem.at[col_number(name, half)]).wait()

    def cross_wait(name, half):
        ref = col(other[name], half)
        pltpu.make_async_copy(ref, ref, rsem.at[cross_number(name, half)]).wait()

    def row_send(k, half, where, lands):
        piece(row(k, half), row(lands, half), row_number(lands, half), where)

    def col_send(name, half, where, lands):
        ref = col(slots[name], half)
        piece(ref, ref, col_number(lands, half), where)

    def cross_send(name, half):
        ref = col(slots[name], half)
        piece(ref, ref, cross_number(name, half), "core")

    mirror = [0, 2, 1, 3, 4, 6, 5, 7]
    for k, peer in enumerate(row_peers, 1):
        at = mirror[k]
        send(id_col, row_ids.at[at], isend.at[k - 1], irecv.at[at - 1], peer)
    for k, peer in enumerate(col_peers, 1):
        send(id_row, col_ids.at[own], isend.at[6 + k], irecv.at[6 + mirror[k]], peer)
    for k, peer in enumerate(cross_peers):
        send(id_row, col_ids.at[own], isend.at[14 + k], irecv.at[14 + mirror[k]], peer)

    for half in range(2):
        row_send(0, half, "zr", 4)
        col_send("own", half, "zc", "zc")
        row_send(0, half, "x+", 1)
        row_send(0, half, "x-", 2)
        col_send("own", half, "y+", "ym")
        col_send("own", half, "y-", "yp")
        cross_send("own", half)
    for half in range(2):
        row_wait(4, half)
        row_send(4, half, "x+", 5)
        row_send(4, half, "x-", 6)
        col_wait("zc", half)
        col_send("zc", half, "y+", "zcym")
        col_send("zc", half, "y-", "zcyp")
        cross_send("zc", half)
    row_wait(1, 0)
    row_send(1, 0, "x+", 3)
    row_wait(2, 0)
    col_wait("ym", 0)
    col_send("ym", 0, "y+", "y2")
    cross_send("ym", 0)
    col_wait("yp", 0)
    cross_send("yp", 0)
    row_wait(2, 1)
    row_send(2, 1, "x-", 3)
    row_wait(1, 1)
    col_wait("yp", 1)
    col_send("yp", 1, "y-", "y2")
    cross_send("yp", 1)
    col_wait("ym", 1)
    cross_send("ym", 1)
    for half in range(2):
        for k in (5, 6):
            row_wait(k, half)
        for name in ("zcym", "zcyp"):
            col_wait(name, half)
            cross_send(name, half)
    for half in range(2):
        row_wait(3, half)
        row_send(3, half, "zr", 7)
        col_wait("y2", half)
        col_send("y2", half, "zc", "zcy2")
        cross_send("y2", half)
    for half in range(2):
        col_wait("zcy2", half)
        cross_send("zcy2", half)
        row_wait(7, half)

    for number in range(7):
        ref = row_ids.at[number + 1]
        pltpu.make_async_copy(ref, ref, irecv.at[number]).wait()
    for number, name in enumerate(col_names[1:]):
        ref = col_ids.at[slots[name]]
        pltpu.make_async_copy(ref, ref, irecv.at[7 + number]).wait()
    for number, name in enumerate(col_names):
        ref = col_ids.at[other[name]]
        pltpu.make_async_copy(ref, ref, irecv.at[14 + number]).wait()
    for name in col_names:
        for half in range(2):
            cross_wait(name, half)

    mine = x * 2 + lax.div(z, 2)

    def score(tile, carry):
        block = pl.ds(tile * 4, 4)
        products = lax.dot_general(
            rowbuf[...].reshape(256, 4096),
            colbuf[block].reshape(128, 4096),
            NT,
            preferred_element_type=F32,
        )
        ids = jnp.sum(col_ids[block], axis=0)[:1]
        for k in range(8):
            part = products[k * 32 : (k + 1) * 32] * factor
            part = jnp.where(row_ids[k] == ids, 0.0, part).astype(BF)
            res_send[k, :, pl.ds(pl.multiple_of(tile * 128, 128), 128)] = part
        return carry

    lax.fori_loop(0, 4, score, 0)
    for k, peer in enumerate(row_peers, 1):
        at = mirror[k] - 1
        send(res_send.at[k], res_recv.at[mine], osend.at[k - 1], orecv.at[at], peer)
    res_recv[mine] = res_send[0]
    for number in range(7):
        a, b = row_places[number + 1]
        ref = res_recv.at[a * 2 + lax.div(b, 2)]
        pltpu.make_async_copy(ref, ref, orecv.at[number]).wait()
    for index in range(8):
        xi, k = index // 2, index % 2
        for yi in range(4):
            at = (xi // 2) * 2048 + yi * 512 + (xi % 2) * 256 + k * 128
            out_ref[:, at : at + 128] = res_recv[index, :, yi * 128 : (yi + 1) * 128].astype(F32)
    for copy in started:
        copy.wait_send()


def scores(feat, ids, factor):
    return pl.pallas_call(
        functools.partial(score_kernel, factor=factor),
        out_shape=jax.ShapeDtypeStruct((32, 4096), F32),
        in_specs=[pl.BlockSpec(memory_space=pl.ANY), pl.BlockSpec(memory_space=pltpu.SMEM)],
        out_specs=pl.BlockSpec(memory_space=pltpu.VMEM),
        scratch_shapes=[
            pltpu.VMEM((8, 2, 16, 4096), BF),
            pltpu.VMEM((16, 2, 16, 4096), BF),
            pltpu.VMEM((8, 32, 512), BF),
            pltpu.VMEM((8, 32, 512), BF),
            pltpu.VMEM((32, 128), jnp.int32),
            pltpu.VMEM((8, 128), jnp.int32),
            pltpu.VMEM((8, 32, 128), jnp.int32),
            pltpu.VMEM((16, 8, 128), jnp.int32),
            pltpu.SemaphoreType.DMA((2,)),
            pltpu.SemaphoreType.DMA((44,)),
            pltpu.SemaphoreType.DMA((44,)),
            pltpu.SemaphoreType.DMA((22,)),
            pltpu.SemaphoreType.DMA((22,)),
            pltpu.SemaphoreType.DMA((7,)),
            pltpu.SemaphoreType.DMA((7,)),
        ],
        compiler_params=pltpu.CompilerParams(
            collective_id=0, has_side_effects=True, vmem_limit_bytes=48 << 20
        ),
        name="scores",
    )(feat, ids)


def on_device(activations, out_grads, proj_in, proj_out, basis_in, basis_out, eigen, doc_ids):
    local_count, tokens, width = activations.shape
    rank = proj_in.shape[1]
    feat = features(
        activations.reshape(-1, width), out_grads.reshape(-1, width),
        proj_in.T, proj_out.T, basis_in, basis_out, eigen,
    )
    return scores(feat, doc_ids, 1.0 / (tokens * rank))


def solution(mesh):
    return jax.shard_map(
        on_device,
        mesh=mesh,
        in_specs=(
            P(("grp", "mem"), None, None),
            P(("grp", "mem"), None, None),
            P(),
            P(),
            P(),
            P(),
            P(),
            P(("grp", "mem")),
        ),
        out_specs=P(("grp", "mem"), None),
        check_vma=False,
    )
```

time: 284 us -> 65.8 us (0.23)
  waiting for transfers between devices: 168 us -> 0 us
  blocking collectives: 68.7 us -> 0 us
  Pallas kernels: 0 us -> 63.8 us
  matrix products: 30.5 us -> 0 us
  between operations: 13.5 us -> 0.03 us
    all_gather x1 -> x0, waiting for transfers between devices: 168 us -> none  [on_device(): lax.all_gather(scaled, ('grp', 'mem'), axis=0, tiled=True)]
    unnamed x1 -> x0, blocking collectives: 68.7 us -> none
    pallas_call x0 -> x2, Pallas kernels: none -> 63.8 us  [the longest x1 44.7 us: scores(): pl.pallas_call(functools.partial(score_kernel, factor=factor), out_shape=...]
    dot_general x6 -> x0, matrix products: 30.5 us -> none  [the longest x1 16 us: score_block(): lax.dot_general(own_feat, other_feat, (((1,), (1,)), ((), ())), preferred...]
  transfers between devices with their start and end apart: 1 -> 0, of which waited for: 1 -> 0; matrix products, arithmetic and copies ran while one was open for 0% -> 0% of each run, Pallas kernels for 0% -> 0%
where the time goes in v1:
time: 65.8 us; the launch traced here: 65.6 us
  Pallas kernels  63.8 us (97%)
  local copies, waits for them, and re-layouts  1.74 us (3%)
    pallas_call x1, Pallas kernels, scores(): pl.pallas_call(functools.partial(score_kernel, factor=factor), out_shape=...  44.7 us
    pallas_call x1, Pallas kernels, features(): pl.pallas_call(feature_kernel, out_shape=jax.ShapeDtypeStruct((2, 16, 409...  19.1 us
    unnamed x5, local copies, waits for them, and re-layouts  1.74 us

profile of v1, /device:TPU:1, one launch (start us, length us, event | category | flops | bytes accessed | tf_op | source)
XLA Modules:
  0.0 65.6 jit_solution(10701921304403898759)
XLA Ops:
  0.0 0.0 copy-start.1
  0.0 19.1 %features.1.feat_hbm = bf16[2,16,4096]{2,1,0:T(8,128)(2,1)} custom-call(bf16[1024,4096]{1,0:T(8,128)(2,1)} %bitcast.4, bf16[1024,4096]{1,0:T(8,128)(2,1)} %bitcast.5, bf16[64,4096]{1,0:T(8,128)(2,1)} %bitcast.6, bf16[64,4096]{1,0:T(8,128)(2,1)} %bitcast.7, f32[64,64]{1,0:T(8,128)} %bin_ref.1, f32[64,64]{1,0:T(8,128)} %bout_ref.1, f32[64,64]{1,0:T(8,128)} %eig_ref.1), custom_call_target="tpu_custom_call" | custom-call | tf_op jit(solution)/shard_map/features/pallas_call | solution.py:110
  19.1 0.0 copy-done.1
  19.2 0.0 copy-start
  19.2 0.9 %copy-done = bf16[2,16,4096]{2,1,0:T(8,128)(2,1)S(1)} copy-done((bf16[2,16,4096]{2,1,0:T(8,128)(2,1)S(1)}, bf16[2,16,4096]{2,1,0:T(8,128)(2,1)}, u32[]{:S(2)}) %copy-start) | copy-done | bytes 262168
  20.1 44.7 %scores.1 = f32[32,4096]{1,0:T(8,128)S(1)} custom-call(bf16[2,16,4096]{2,1,0:T(8,128)(2,1)S(1)} %copy-done, s32[32]{0:T(128)S(1)} %copy-done.1), custom_call_target="tpu_custom_call" | custom-call | tf_op jit(solution)/shard_map/scores/pallas_call | solution.py:360
  64.8 0.8 %copy.10 = f32[32,4096]{1,0:T(8,128)} copy(f32[32,4096]{1,0:T(8,128)S(1)} %scores.1) | data formatting | bytes 1048576
Async XLA Ops:
  0.0 19.1 %copy-start.1 = (s32[32]{0:T(128)S(1)}, s32[32]{0:T(128)}, u32[]{:S(2)}) copy-start(s32[32]{0:T(128)} %ids_ref.1) | copy-start | bytes 388
  19.2 1.0 %copy-start = (bf16[2,16,4096]{2,1,0:T(8,128)(2,1)S(1)}, bf16[2,16,4096]{2,1,0:T(8,128)(2,1)}, u32[]{:S(2)}) copy-start(bf16[2,16,4096]{2,1,0:T(8,128)(2,1)} %features.1.feat_hbm) | copy-start | bytes 786436

commit v2 on v0

v2 whole, which is shorter than its diff:
```python
import functools

import jax
import jax.numpy as jnp
from jax import lax
from jax.experimental import pallas as pl
from jax.experimental.pallas import tpu as pltpu
from jax.sharding import PartitionSpec as P

damping = 0.1
BF = jnp.bfloat16
F32 = jnp.float32
MESH = pl.DeviceIdType.MESH
NT = (((1,), (1,)), ((), ()))


def dot(a, b):
    return jnp.dot(a, b, preferred_element_type=F32)


def split(value):
    high = value.astype(BF)
    return high, (value - high.astype(F32)).astype(BF)


def kernel(
    act_hbm, grad_hbm, pin_hbm, pout_hbm, bin_hbm, bout_hbm, eig_hbm, ids_hbm, out_ref,
    act, grad, w_in, w_out, b_in, b_out, eig, ids_ref, w_g, scale,
    rowbuf, colbuf, res_send, res_recv, id_col, id_row, row_ids, col_ids,
    dsem, wsem, ssem, rsem, isend, irecv, osend, orecv,
    *, factor,
):
    g = lax.axis_index("grp")
    m = lax.axis_index("mem")
    x = lax.div(g, 4) * 2 + lax.div(m, 8)
    y = lax.rem(g, 4)
    z = lax.rem(lax.div(m, 2), 4)
    c = lax.rem(m, 2)
    odd = lax.rem(z, 2)
    zr = lax.rem(z + 3 + 2 * odd, 4)
    zc = z + 1 - 2 * odd
    xm, xp, x2 = lax.rem(x + 3, 4), lax.rem(x + 1, 4), lax.rem(x + 2, 4)
    ym, yp, y2 = lax.rem(y + 3, 4), lax.rem(y + 1, 4), lax.rem(y + 2, 4)
    oc = 1 - c

    def device(x, y, z, c):
        return (lax.div(x, 2) * 4 + y, lax.rem(x, 2) * 8 + z * 2 + c)

    def slot(y, z, c):
        return y * 4 + lax.rem(z, 2) * 2 + c

    row_places = [(a, b) for b in (z, zr) for a in (x, xm, xp, x2)]
    row_peers = [device(a, y, b, c) for a, b in row_places[1:]]
    col_places = [(a, b) for b in (z, zc) for a in (y, ym, yp, y2)]
    col_peers = [device(x, a, b, c) for a, b in col_places[1:]]
    cross_peers = [device(x, a, b, oc) for a, b in col_places]
    own = slot(y, z, c)

    weights = [
        pltpu.make_async_copy(src, dst, wsem.at[number])
        for number, (src, dst) in enumerate(
            [
                (bout_hbm, b_out), (bin_hbm, b_in), (eig_hbm, eig), (ids_hbm, ids_ref),
                (pin_hbm, w_in), (pout_hbm, w_out),
            ]
        )
    ]
    loads = []
    for part in range(4):
        rows = pl.ds(part * 256, 256)
        loads.append(
            (
                pltpu.make_async_copy(act_hbm.at[rows], act.at[rows], dsem.at[part]),
                pltpu.make_async_copy(grad_hbm.at[rows], grad.at[rows], dsem.at[4 + part]),
            )
        )
    for copy in weights:
        copy.start()
    for part in range(2):
        for copy in loads[part]:
            copy.start()
    barrier = pltpu.get_barrier_semaphore()
    everyone = row_peers + col_peers + cross_peers
    for peer in everyone:
        pl.semaphore_signal(barrier, inc=1, device_id=peer, device_id_type=MESH)

    for copy in weights[:4]:
        copy.wait()
    zeros = jnp.zeros((64, 64), BF)
    out_high, out_low = split(b_out[...])
    stacked = jnp.concatenate([zeros, out_high, zeros, out_low], axis=0)
    for tile in range(16):
        unit = lax.broadcasted_iota(jnp.int32, (64, 256), 0)
        lane = lax.broadcasted_iota(jnp.int32, (64, 256), 1)
        spread = jnp.where(lax.div(lane, 64) + tile * 4 == unit, 1.0, 0.0).astype(BF)
        w_g[:, tile * 256 : (tile + 1) * 256] = dot(stacked, spread).astype(BF)
    in_high, in_low = split(b_in[...])
    wide_zeros = jnp.zeros((64, 128), BF)
    w_a = jnp.concatenate(
        [
            jnp.concatenate([in_high, in_high], axis=1),
            wide_zeros,
            jnp.concatenate([in_low, in_low], axis=1),
            wide_zeros,
        ],
        axis=0,
    )
    inverse = 1.0 / jnp.sqrt(eig[...] + damping)
    for tile in range(32):
        scale[:, tile * 128 : (tile + 1) * 128] = jnp.concatenate(
            [inverse[2 * tile : 2 * tile + 1], inverse[2 * tile + 1 : 2 * tile + 2]], axis=1
        )
    row_at = lax.broadcasted_iota(jnp.int32, (256, 256), 0)
    col_at = lax.broadcasted_iota(jnp.int32, (256, 256), 1)
    perm = jnp.where(
        lax.rem(row_at, 8) * 32 + lax.div(row_at, 8) == col_at, 1.0, 0.0
    ).astype(BF)

    lane = lax.broadcasted_iota(jnp.int32, (8, 128), 1)
    first = (odd * 2 + c) * 32
    placed = jnp.zeros((8, 128), jnp.int32)
    for example in range(32):
        value = ids_ref[example]
        placed = jnp.where(lane == first + example, value, placed)
        id_col[example : example + 1, :] = jnp.full((1, 128), value, jnp.int32)
    id_row[...] = placed
    row_ids[0] = id_col[...]
    col_ids[own] = placed

    started = []

    def send(src, dst, send_sem, recv_sem, peer):
        copy = pltpu.make_async_remote_copy(
            src_ref=src, dst_ref=dst, send_sem=send_sem, recv_sem=recv_sem,
            device_id=peer, device_id_type=MESH,
        )
        copy.start()
        started.append(copy)

    to = {
        "x+": device(xp, y, z, c), "x-": device(xm, y, z, c),
        "y+": device(x, yp, z, c), "y-": device(x, ym, z, c),
        "zr": device(x, y, zr, c), "zc": device(x, y, zc, c),
        "core": device(x, y, z, oc),
    }
    count = [0]

    def piece(src, dst, number, where):
        send(src, dst, ssem.at[count[0]], rsem.at[number], to[where])
        count[0] += 1

    def row(k, q):
        return rowbuf.at[k, pl.ds(q * 8, 8)]

    def col(index, q):
        return colbuf.at[index, pl.ds(q * 8, 8)]

    col_names = ["own", "ym", "yp", "y2", "zc", "zcym", "zcyp", "zcy2"]
    row_names = ["own", "xm", "xp", "x2", "zr", "zrxm", "zrxp", "zrx2"]

    def row_number(name, q):
        return (row_names.index(name) - 1) * 4 + q

    def col_number(name, q):
        return 28 + (col_names.index(name) - 1) * 4 + q

    def cross_number(name, q):
        return 56 + col_names.index(name) * 4 + q

    slots = {name: slot(a, b, c) for name, (a, b) in zip(col_names, col_places)}
    other = {name: slot(a, b, oc) for name, (a, b) in zip(col_names, col_places)}

    def row_wait(name, q):
        ref = row(row_names.index(name), q)
        pltpu.make_async_copy(ref, ref, rsem.at[row_number(name, q)]).wait()

    def col_wait(name, q):
        ref = col(slots[name], q)
        pltpu.make_async_copy(ref, ref, rsem.at[col_number(name, q)]).wait()

    def cross_wait(name, q):
        ref = col(other[name], q)
        pltpu.make_async_copy(ref, ref, rsem.at[cross_number(name, q)]).wait()

    def row_send(name, q, where, lands):
        src, dst = row(row_names.index(name), q), row(row_names.index(lands), q)
        piece(src, dst, row_number(lands, q), where)

    def col_send(name, q, where, lands):
        ref = col(slots[name], q)
        piece(ref, ref, col_number(lands, q), where)

    def cross_send(name, q):
        ref = col(slots[name], q)
        piece(ref, ref, cross_number(name, q), "core")

    def own_out(q):
        row_send("own", q, "zr", "zr")
        col_send("own", q, "zc", "zc")
        row_send("own", q, "x+", "xm")
        row_send("own", q, "x-", "xp")
        col_send("own", q, "y+", "ym")
        col_send("own", q, "y-", "yp")
        cross_send("own", q)

    def z_on(q):
        row_wait("zr", q)
        row_send("zr", q, "x+", "zrxm")
        row_send("zr", q, "x-", "zrxp")
        col_wait("zc", q)
        col_send("zc", q, "y+", "zcym")
        col_send("zc", q, "y-", "zcyp")
        cross_send("zc", q)

    def far_on(q):
        row_wait("xm", q)
        row_wait("xp", q)
        if q < 2:
            row_send("xm", q, "x+", "x2")
        else:
            row_send("xp", q, "x-", "x2")
        col_wait("ym", q)
        col_wait("yp", q)
        if q < 2:
            col_send("ym", q, "y+", "y2")
        else:
            col_send("yp", q, "y-", "y2")
        cross_send("ym", q)
        cross_send("yp", q)

    mirror = [0, 2, 1, 3, 4, 6, 5, 7]
    for copy in weights[4:]:
        copy.wait()
    for part in range(4):
        for copy in loads[part]:
            copy.wait()
        if part < 2:
            for copy in loads[part + 2]:
                copy.start()
        rows = pl.ds(part * 256, 256)
        projected = jnp.concatenate(
            [
                lax.dot_general(act[rows, :], w_in[...], NT, preferred_element_type=F32),
                lax.dot_general(grad[rows, :], w_out[...], NT, preferred_element_type=F32),
            ],
            axis=1,
        )
        moved = dot(perm, projected.astype(BF)).astype(BF)
        pair = jnp.concatenate([moved, moved], axis=1)
        rotated = dot(pair, w_a)
        twice = jnp.concatenate([rotated, rotated], axis=1)
        for tile in range(16):
            lanes = slice(tile * 256, (tile + 1) * 256)
            product = dot(pair, w_g[:, lanes]) * twice
            feature = jnp.sum(product.reshape(32, 8, 256), axis=0) * scale[:, lanes]
            feature = feature.astype(BF)
            rowbuf[0, part * 8 : (part + 1) * 8, lanes] = feature
            colbuf[own, part * 8 : (part + 1) * 8, lanes] = feature
        if part == 0:
            pl.semaphore_wait(barrier, len(everyone))
            for k, peer in enumerate(row_peers, 1):
                at = mirror[k]
                send(id_col, row_ids.at[at], isend.at[k - 1], irecv.at[at - 1], peer)
            for k, peer in enumerate(col_peers, 1):
                send(id_row, col_ids.at[own], isend.at[6 + k], irecv.at[6 + mirror[k]], peer)
            for k, peer in enumerate(cross_peers):
                send(id_row, col_ids.at[own], isend.at[14 + k], irecv.at[14 + mirror[k]], peer)
        else:
            z_on(part - 1)
        own_out(part)
        if part >= 2:
            far_on(part - 2)
    z_on(3)
    far_on(2)
    far_on(3)
    for q in range(4):
        for name in ("zcym", "zcyp"):
            col_wait(name, q)
            cross_send(name, q)
        for name in ("zrxm", "zrxp"):
            row_wait(name, q)
    for q in (0, 2, 1, 3):
        row_wait("x2", q)
        row_send("x2", q, "zr", "zrx2")
        col_wait("y2", q)
        col_send("y2", q, "zc", "zcy2")
        cross_send("y2", q)
    for q in (0, 2, 1, 3):
        col_wait("zcy2", q)
        cross_send("zcy2", q)
        row_wait("zrx2", q)

    for k in range(1, 8):
        ref = row_ids.at[k]
        pltpu.make_async_copy(ref, ref, irecv.at[k - 1]).wait()
    for k, name in enumerate(col_names):
        if k:
            ref = col_ids.at[slots[name]]
            pltpu.make_async_copy(ref, ref, irecv.at[6 + k]).wait()
        ref = col_ids.at[other[name]]
        pltpu.make_async_copy(ref, ref, irecv.at[14 + k]).wait()
    for name in col_names:
        for q in range(4):
            cross_wait(name, q)

    mine = x * 2 + lax.div(z, 2)
    for half in range(2):
        block = pl.ds(half * 8, 8)
        products = lax.dot_general(
            rowbuf[...].reshape(256, 4096),
            colbuf[block].reshape(256, 4096),
            NT,
            preferred_element_type=F32,
        )
        ids = jnp.concatenate(
            [
                jnp.sum(col_ids[pl.ds(half * 8 + 4 * part, 4)], axis=0)[:1]
                for part in range(2)
            ],
            axis=1,
        )
        for k in range(8):
            part = products[k * 32 : (k + 1) * 32] * factor
            same = jnp.concatenate([row_ids[k], row_ids[k]], axis=1) == ids
            res_send[k, :, half * 256 : (half + 1) * 256] = jnp.where(same, 0.0, part).astype(BF)
    for k, peer in enumerate(row_peers, 1):
        at = mirror[k] - 1
        send(res_send.at[k], res_recv.at[mine], osend.at[k - 1], orecv.at[at], peer)
    res_recv[mine] = res_send[0]
    for number in range(7):
        a, b = row_places[number + 1]
        ref = res_recv.at[a * 2 + lax.div(b, 2)]
        pltpu.make_async_copy(ref, ref, orecv.at[number]).wait()
    for index in range(8):
        xi, k = index // 2, index % 2
        for yi in range(4):
            at = (xi // 2) * 2048 + yi * 512 + (xi % 2) * 256 + k * 128
            out_ref[:, at : at + 128] = res_recv[index, :, yi * 128 : (yi + 1) * 128].astype(F32)
    for copy in started:
        copy.wait_send()


def on_device(activations, out_grads, proj_in, proj_out, basis_in, basis_out, eigen, doc_ids):
    local_count, tokens, width = activations.shape
    rank = proj_in.shape[1]
    return pl.pallas_call(
        functools.partial(kernel, factor=1.0 / (tokens * rank)),
        out_shape=jax.ShapeDtypeStruct((32, 4096), F32),
        in_specs=[pl.BlockSpec(memory_space=pl.ANY)] * 8,
        out_specs=pl.BlockSpec(memory_space=pltpu.VMEM),
        scratch_shapes=[
            pltpu.VMEM((1024, 4096), BF),
            pltpu.VMEM((1024, 4096), BF),
            pltpu.VMEM((64, 4096), BF),
            pltpu.VMEM((64, 4096), BF),
            pltpu.VMEM((64, 64), F32),
            pltpu.VMEM((64, 64), F32),
            pltpu.VMEM((64, 64), F32),
            pltpu.SMEM((32,), jnp.int32),
            pltpu.VMEM((256, 4096), BF),
            pltpu.VMEM((1, 4096), F32),
            pltpu.VMEM((8, 32, 4096), BF),
            pltpu.VMEM((16, 32, 4096), BF),
            pltpu.VMEM((8, 32, 512), BF),
            pltpu.VMEM((8, 32, 512), BF),
            pltpu.VMEM((32, 128), jnp.int32),
            pltpu.VMEM((8, 128), jnp.int32),
            pltpu.VMEM((8, 32, 128), jnp.int32),
            pltpu.VMEM((16, 8, 128), jnp.int32),
            pltpu.SemaphoreType.DMA((8,)),
            pltpu.SemaphoreType.DMA((6,)),
            pltpu.SemaphoreType.DMA((88,)),
            pltpu.SemaphoreType.DMA((88,)),
            pltpu.SemaphoreType.DMA((22,)),
            pltpu.SemaphoreType.DMA((22,)),
            pltpu.SemaphoreType.DMA((7,)),
            pltpu.SemaphoreType.DMA((7,)),
        ],
        compiler_params=pltpu.CompilerParams(
            collective_id=0, has_side_effects=True, vmem_limit_bytes=60 << 20
        ),
        name="influence",
    )(
        activations.reshape(-1, width), out_grads.reshape(-1, width),
        proj_in.T, proj_out.T, basis_in, basis_out, eigen, doc_ids,
    )


def solution(mesh):
    return jax.shard_map(
        on_device,
        mesh=mesh,
        in_specs=(
            P(("grp", "mem"), None, None),
            P(("grp", "mem"), None, None),
            P(),
            P(),
            P(),
            P(),
            P(),
            P(("grp", "mem")),
        ),
        out_specs=P(("grp", "mem"), None),
        check_vma=False,
    )
```

time: 284 us -> 50.5 us (0.18)
  waiting for transfers between devices: 168 us -> 0 us
  blocking collectives: 68.7 us -> 0 us
  Pallas kernels: 0 us -> 48.5 us
  matrix products: 30.5 us -> 0 us
  between operations: 13.5 us -> 0.01 us
    all_gather x1 -> x0, waiting for transfers between devices: 168 us -> none  [on_device(): lax.all_gather(scaled, ('grp', 'mem'), axis=0, tiled=True)]
    unnamed x1 -> x0, blocking collectives: 68.7 us -> none
    pallas_call x0 -> x1, Pallas kernels: none -> 48.5 us  [on_device(): pl.pallas_call(functools.partial(kernel, factor=1.0 / (tokens * rank)), o...]
    dot_general x6 -> x0, matrix products: 30.5 us -> none  [the longest x1 16 us: score_block(): lax.dot_general(own_feat, other_feat, (((1,), (1,)), ((), ())), preferred...]
  transfers between devices with their start and end apart: 1 -> 0, of which waited for: 1 -> 0; matrix products, arithmetic and copies ran while one was open for 0% -> 0% of each run, Pallas kernels for 0% -> 0%
where the time goes in v2:
time: 50.5 us; the launch traced here: 50.4 us
  Pallas kernels  48.5 us (96%)
  local copies, waits for them, and re-layouts  1.87 us (4%)
    pallas_call x1, Pallas kernels, on_device(): pl.pallas_call(functools.partial(kernel, factor=1.0 / (tokens * rank)), o...  48.5 us
    unnamed x1, local copies, waits for them, and re-layouts  1.87 us

profile of v2, /device:TPU:1, one launch (start us, length us, event | category | flops | bytes accessed | tf_op | source)
XLA Modules:
  0.0 50.4 jit_solution(12067830582822933670)
XLA Ops:
  0.0 48.5 %influence.1 = f32[32,4096]{1,0:T(8,128)} custom-call(bf16[1024,4096]{1,0:T(8,128)(2,1)} %bitcast.4, bf16[1024,4096]{1,0:T(8,128)(2,1)} %bitcast.5, bf16[64,4096]{1,0:T(8,128)(2,1)} %bitcast.6, bf16[64,4096]{1,0:T(8,128)(2,1)} %bitcast.7, f32[64,64]{1,0:T(8,128)} %bin_hbm.1, f32[64,64]{1,0:T(8,128)} %bout_hbm.1, f32[64,64]{1,0:T(8,128)} %eig_hbm.1, s32[32]{0:T(128)} %ids_hbm.1), custom_call_target="tpu_custom_call" | custom-call | tf_op jit(solution)/shard_map/influence/pallas_call | solution.py:346
  48.5 1.9 %copy.10 = f32[32,4096]{1,0:T(8,128)} copy(f32[32,4096]{1,0:T(8,128)} %influence.1) | data formatting | bytes 1048576

commit v3 on v2

--- a/solution.py
+++ b/solution.py
@@ -76,9 +76,8 @@
         )
     for copy in weights:
         copy.start()
-    for part in range(2):
-        for copy in loads[part]:
-            copy.start()
+    for copy in loads[0]:
+        copy.start()
     barrier = pltpu.get_barrier_semaphore()
     everyone = row_peers + col_peers + cross_peers
     for peer in everyone:
@@ -86,6 +85,8 @@
 
     for copy in weights[:4]:
         copy.wait()
+    for copy in loads[1]:
+        copy.start()
     zeros = jnp.zeros((64, 64), BF)
     out_high, out_low = split(b_out[...])
     stacked = jnp.concatenate([zeros, out_high, zeros, out_low], axis=0)
@@ -203,53 +204,69 @@
         col_send("own", q, "y-", "yp")
         cross_send("own", q)
 
-    def z_on(q):
+    def mid_on(q):
+        near = ("xm", "x+", "ym", "y+") if q % 2 == 0 else ("xp", "x-", "yp", "y-")
+        row_wait(near[0], q)
+        row_send(near[0], q, near[1], "x2")
+        col_wait(near[2], q)
+        col_send(near[2], q, near[3], "y2")
         row_wait("zr", q)
         row_send("zr", q, "x+", "zrxm")
         row_send("zr", q, "x-", "zrxp")
         col_wait("zc", q)
         col_send("zc", q, "y+", "zcym")
         col_send("zc", q, "y-", "zcyp")
-        cross_send("zc", q)
-
-    def far_on(q):
-        row_wait("xm", q)
-        row_wait("xp", q)
-        if q < 2:
-            row_send("xm", q, "x+", "x2")
-        else:
-            row_send("xp", q, "x-", "x2")
-        col_wait("ym", q)
-        col_wait("yp", q)
-        if q < 2:
-            col_send("ym", q, "y+", "y2")
-        else:
-            col_send("yp", q, "y-", "y2")
-        cross_send("ym", q)
-        cross_send("yp", q)
+        row_wait("xp" if q % 2 == 0 else "xm", q)
+        col_wait("yp" if q % 2 == 0 else "ym", q)
+        for name in ("zc", "ym", "yp"):
+            cross_send(name, q)
+
+    def last_on(q):
+        row_wait("x2", q)
+        row_send("x2", q, "zr", "zrx2")
+        col_wait("y2", q)
+        col_send("y2", q, "zc", "zcy2")
+        cross_send("y2", q)
+
+    def side_on(q):
+        for name in ("zcym", "zcyp"):
+            col_wait(name, q)
+            cross_send(name, q)
+        for name in ("zrxm", "zrxp"):
+            row_wait(name, q)
 
     mirror = [0, 2, 1, 3, 4, 6, 5, 7]
-    for copy in weights[4:]:
+    def project(part, piece_at, pieces):
+        rows = pl.ds(part * 256, 256)
+        deep = slice(piece_at * 4096 // pieces, (piece_at + 1) * 4096 // pieces)
+        return (
+            lax.dot_general(act[rows, deep], w_in[:, deep], NT, preferred_element_type=F32),
+            lax.dot_general(grad[rows, deep], w_out[:, deep], NT, preferred_element_type=F32),
+        )
+
+    for copy in weights[4:] + list(loads[0]):
         copy.wait()
+    for copy in loads[2]:
+        copy.start()
+    sums = project(0, 0, 1)
+    pieces = 4
     for part in range(4):
-        for copy in loads[part]:
-            copy.wait()
-        if part < 2:
-            for copy in loads[part + 2]:
+        if part < 3:
+            for copy in loads[part + 1]:
+                copy.wait()
+        if part == 0:
+            for copy in loads[3]:
                 copy.start()
-        rows = pl.ds(part * 256, 256)
-        projected = jnp.concatenate(
-            [
-                lax.dot_general(act[rows, :], w_in[...], NT, preferred_element_type=F32),
-                lax.dot_general(grad[rows, :], w_out[...], NT, preferred_element_type=F32),
-            ],
-            axis=1,
-        )
+        projected = jnp.concatenate(sums, axis=1)
         moved = dot(perm, projected.astype(BF)).astype(BF)
         pair = jnp.concatenate([moved, moved], axis=1)
         rotated = dot(pair, w_a)
         twice = jnp.concatenate([rotated, rotated], axis=1)
+        sums = None
         for tile in range(16):
+            if part < 3 and tile % (16 // pieces) == 0:
+                more = project(part + 1, tile * pieces // 16, pieces)
+                sums = more if sums is None else (sums[0] + more[0], sums[1] + more[1])
             lanes = slice(tile * 256, (tile + 1) * 256)
             product = dot(pair, w_g[:, lanes]) * twice
             feature = jnp.sum(product.reshape(32, 8, 256), axis=0) * scale[:, lanes]
@@ -258,6 +275,8 @@
             colbuf[own, part * 8 : (part + 1) * 8, lanes] = feature
         if part == 0:
             pl.semaphore_wait(barrier, len(everyone))
+        own_out(part)
+        if part == 0:
             for k, peer in enumerate(row_peers, 1):
                 at = mirror[k]
                 send(id_col, row_ids.at[at], isend.at[k - 1], irecv.at[at - 1], peer)
@@ -265,27 +284,19 @@
                 send(id_row, col_ids.at[own], isend.at[6 + k], irecv.at[6 + mirror[k]], peer)
             for k, peer in enumerate(cross_peers):
                 send(id_row, col_ids.at[own], isend.at[14 + k], irecv.at[14 + mirror[k]], peer)
-        else:
-            z_on(part - 1)
-        own_out(part)
         if part >= 2:
-            far_on(part - 2)
-    z_on(3)
-    far_on(2)
-    far_on(3)
+            mid_on(part - 2)
+    mid_on(2)
+    last_on(0)
+    mid_on(3)
+    last_on(1)
+    side_on(0)
+    side_on(1)
+    last_on(2)
+    side_on(2)
+    last_on(3)
+    side_on(3)
     for q in range(4):
-        for name in ("zcym", "zcyp"):
-            col_wait(name, q)
-            cross_send(name, q)
-        for name in ("zrxm", "zrxp"):
-            row_wait(name, q)
-    for q in (0, 2, 1, 3):
-        row_wait("x2", q)
-        row_send("x2", q, "zr", "zrx2")
-        col_wait("y2", q)
-        col_send("y2", q, "zc", "zcy2")
-        cross_send("y2", q)
-    for q in (0, 2, 1, 3):
         col_wait("zcy2", q)
         cross_send("zcy2", q)
         row_wait("zrx2", q)
@@ -322,20 +333,26 @@
         for k in range(8):
             part = products[k * 32 : (k + 1) * 32] * factor
             same = jnp.concatenate([row_ids[k], row_ids[k]], axis=1) == ids
-            res_send[k, :, half * 256 : (half + 1) * 256] = jnp.where(same, 0.0, part).astype(BF)
-    for k, peer in enumerate(row_peers, 1):
-        at = mirror[k] - 1
-        send(res_send.at[k], res_recv.at[mine], osend.at[k - 1], orecv.at[at], peer)
-    res_recv[mine] = res_send[0]
-    for number in range(7):
-        a, b = row_places[number + 1]
-        ref = res_recv.at[a * 2 + lax.div(b, 2)]
-        pltpu.make_async_copy(ref, ref, orecv.at[number]).wait()
-    for index in range(8):
-        xi, k = index // 2, index % 2
-        for yi in range(4):
-            at = (xi // 2) * 2048 + yi * 512 + (xi % 2) * 256 + k * 128
-            out_ref[:, at : at + 128] = res_recv[index, :, yi * 128 : (yi + 1) * 128].astype(F32)
+            res_send[half, k] = jnp.where(same, 0.0, part).astype(BF)
+        for k in (7, 3, 5, 6, 1, 2, 4):
+            at = half * 7 + mirror[k] - 1
+            send(
+                res_send.at[half, k], res_recv.at[half, mine],
+                osend.at[half * 7 + k - 1], orecv.at[at], row_peers[k - 1],
+            )
+        res_recv[half, mine] = res_send[half, 0]
+    for half in range(2):
+        for k in range(1, 8):
+            a, b = row_places[k]
+            ref = res_recv.at[half, a * 2 + lax.div(b, 2)]
+            pltpu.make_async_copy(ref, ref, orecv.at[half * 7 + k - 1]).wait()
+        for index in range(8):
+            xi, k = index // 2, index % 2
+            for side in range(2):
+                yi = half * 2 + side
+                at = (xi // 2) * 2048 + yi * 512 + (xi % 2) * 256 + k * 128
+                piece_of = res_recv[half, index, :, side * 128 : (side + 1) * 128]
+                out_ref[:, at : at + 128] = piece_of.astype(F32)
     for copy in started:
         copy.wait_send()
 
@@ -361,8 +378,8 @@
             pltpu.VMEM((1, 4096), F32),
             pltpu.VMEM((8, 32, 4096), BF),
             pltpu.VMEM((16, 32, 4096), BF),
-            pltpu.VMEM((8, 32, 512), BF),
-            pltpu.VMEM((8, 32, 512), BF),
+            pltpu.VMEM((2, 8, 32, 256), BF),
+            pltpu.VMEM((2, 8, 32, 256), BF),
             pltpu.VMEM((32, 128), jnp.int32),
             pltpu.VMEM((8, 128), jnp.int32),
             pltpu.VMEM((8, 32, 128), jnp.int32),
@@ -373,16 +390,16 @@
             pltpu.SemaphoreType.DMA((88,)),
             pltpu.SemaphoreType.DMA((22,)),
             pltpu.SemaphoreType.DMA((22,)),
-            pltpu.SemaphoreType.DMA((7,)),
-            pltpu.SemaphoreType.DMA((7,)),
+            pltpu.SemaphoreType.DMA((14,)),
+            pltpu.SemaphoreType.DMA((14,)),
         ],
         compiler_params=pltpu.CompilerParams(
-            collective_id=0, has_side_effects=True, vmem_limit_bytes=60 << 20
+            collective_id=0, has_side_effects=True, vmem_limit_bytes=54600 << 10
         ),
         name="influence",
     )(
         activations.reshape(-1, width), out_grads.reshape(-1, width),
-        proj_in.T, proj_out.T, basis_in, basis_out, eigen, doc_ids,
+        proj_in.T, proj_out.T, *[pltpu.with_memory_space_constraint(v, pltpu.MemorySpace.HBM) for v in (basis_in, basis_out, eigen, doc_ids)],
     )
 
 

time: 50.5 us -> 43.3 us (0.86)
  Pallas kernels: 48.5 us -> 42.4 us
  local copies, waits for them, and re-layouts: 1.87 us -> 0.8 us
    pallas_call x1, Pallas kernels: 48.5 us -> 42.4 us  [on_device(): pl.pallas_call(functools.partial(kernel, factor=1.0 / (tokens * rank)), o...]
    unnamed x1, local copies, waits for them, and re-layouts: 1.87 us -> 0.8 us
where the time goes in v3:
time: 43.3 us; the launch traced here: 43.2 us
  Pallas kernels  42.4 us (98%)
  local copies, waits for them, and re-layouts  0.8 us (2%)
    pallas_call x1, Pallas kernels, on_device(): pl.pallas_call(functools.partial(kernel, factor=1.0 / (tokens * rank)), o...  42.4 us

profile of v3, /device:TPU:1, one launch (start us, length us, event | category | flops | bytes accessed | tf_op | source)
XLA Modules:
  0.0 43.2 jit_solution(7622830190737242123)
XLA Ops:
  0.0 42.4 %influence.1 = f32[32,4096]{1,0:T(8,128)S(1)} custom-call(bf16[1024,4096]{1,0:T(8,128)(2,1)} %bitcast.4, bf16[1024,4096]{1,0:T(8,128)(2,1)} %bitcast.5, bf16[64,4096]{1,0:T(8,128)(2,1)} %bitcast.6, bf16[64,4096]{1,0:T(8,128)(2,1)} %bitcast.7, f32[64,64]{1,0:T(8,128)} %bin_hbm.1, f32[64,64]{1,0:T(8,128)} %bout_hbm.1, f32[64,64]{1,0:T(8,128)} %eig_hbm.1, ...), custom_call_target="tpu_custom_call" | custom-call | tf_op jit(solution)/shard_map/influence/pallas_call | solution.py:363
  42.4 0.8 %copy.10 = f32[32,4096]{1,0:T(8,128)} copy(f32[32,4096]{1,0:T(8,128)S(1)} %influence.1) | data formatting | bytes 1048576

commit v4 on v3

--- a/solution.py
+++ b/solution.py
@@ -26,7 +26,7 @@
 def kernel(
     act_hbm, grad_hbm, pin_hbm, pout_hbm, bin_hbm, bout_hbm, eig_hbm, ids_hbm, out_ref,
     act, grad, w_in, w_out, b_in, b_out, eig, ids_ref, w_g, scale,
-    rowbuf, colbuf, res_send, res_recv, id_col, id_row, row_ids, col_ids,
+    rowbuf, colbuf, res_send, res_recv, id_row, row_ids, col_ids,
     dsem, wsem, ssem, rsem, isend, irecv, osend, orecv,
     *, factor,
 ):
@@ -123,9 +123,8 @@
     for example in range(32):
         value = ids_ref[example]
         placed = jnp.where(lane == first + example, value, placed)
-        id_col[example : example + 1, :] = jnp.full((1, 128), value, jnp.int32)
     id_row[...] = placed
-    row_ids[0] = id_col[...]
+    row_ids[0] = placed
     col_ids[own] = placed
 
     started = []
@@ -204,22 +203,29 @@
         col_send("own", q, "y-", "yp")
         cross_send("own", q)
 
-    def mid_on(q):
-        near = ("xm", "x+", "ym", "y+") if q % 2 == 0 else ("xp", "x-", "yp", "y-")
+    def far_on(q):
+        even = q % 2 == 0
+        near = ("xm", "x+", "ym", "y+") if even else ("xp", "x-", "yp", "y-")
         row_wait(near[0], q)
         row_send(near[0], q, near[1], "x2")
         col_wait(near[2], q)
         col_send(near[2], q, near[3], "y2")
+        cross_send(near[2], q)
+
+    def z_on(q):
         row_wait("zr", q)
         row_send("zr", q, "x+", "zrxm")
         row_send("zr", q, "x-", "zrxp")
         col_wait("zc", q)
         col_send("zc", q, "y+", "zcym")
         col_send("zc", q, "y-", "zcyp")
+        cross_send("zc", q)
+
+    def rest_on(q):
         row_wait("xp" if q % 2 == 0 else "xm", q)
-        col_wait("yp" if q % 2 == 0 else "ym", q)
-        for name in ("zc", "ym", "yp"):
-            cross_send(name, q)
+        name = "yp" if q % 2 == 0 else "ym"
+        col_wait(name, q)
+        cross_send(name, q)
 
     def last_on(q):
         row_wait("x2", q)
@@ -249,24 +255,21 @@
     for copy in loads[2]:
         copy.start()
     sums = project(0, 0, 1)
-    pieces = 4
     for part in range(4):
-        if part < 3:
+        if 0 < part < 3:
             for copy in loads[part + 1]:
                 copy.wait()
-        if part == 0:
-            for copy in loads[3]:
-                copy.start()
         projected = jnp.concatenate(sums, axis=1)
         moved = dot(perm, projected.astype(BF)).astype(BF)
         pair = jnp.concatenate([moved, moved], axis=1)
         rotated = dot(pair, w_a)
         twice = jnp.concatenate([rotated, rotated], axis=1)
-        sums = None
+        if 0 < part < 3:
+            sums = project(part + 1, 0, 1)
+        if part == 2:
+            far_on(0)
+            z_on(0)
         for tile in range(16):
-            if part < 3 and tile % (16 // pieces) == 0:
-                more = project(part + 1, tile * pieces // 16, pieces)
-                sums = more if sums is None else (sums[0] + more[0], sums[1] + more[1])
             lanes = slice(tile * 256, (tile + 1) * 256)
             product = dot(pair, w_g[:, lanes]) * twice
             feature = jnp.sum(product.reshape(32, 8, 256), axis=0) * scale[:, lanes]
@@ -279,26 +282,37 @@
         if part == 0:
             for k, peer in enumerate(row_peers, 1):
                 at = mirror[k]
-                send(id_col, row_ids.at[at], isend.at[k - 1], irecv.at[at - 1], peer)
+                send(id_row, row_ids.at[at], isend.at[k - 1], irecv.at[at - 1], peer)
             for k, peer in enumerate(col_peers, 1):
                 send(id_row, col_ids.at[own], isend.at[6 + k], irecv.at[6 + mirror[k]], peer)
             for k, peer in enumerate(cross_peers):
                 send(id_row, col_ids.at[own], isend.at[14 + k], irecv.at[14 + mirror[k]], peer)
-        if part >= 2:
-            mid_on(part - 2)
-    mid_on(2)
+        if part == 0:
+            for copy in loads[1]:
+                copy.wait()
+            for copy in loads[3]:
+                copy.start()
+            sums = project(1, 0, 1)
+        if part == 3:
+            far_on(1)
+            z_on(1)
+    far_on(2)
+    rest_on(0)
+    rest_on(1)
+    far_on(3)
     last_on(0)
-    mid_on(3)
+    z_on(2)
     last_on(1)
-    side_on(0)
-    side_on(1)
+    rest_on(2)
+    z_on(3)
     last_on(2)
-    side_on(2)
+    rest_on(3)
     last_on(3)
-    side_on(3)
     for q in range(4):
+        side_on(q)
         col_wait("zcy2", q)
         cross_send("zcy2", q)
+    for q in range(4):
         row_wait("zrx2", q)
 
     for k in range(1, 8):
@@ -310,6 +324,11 @@
             pltpu.make_async_copy(ref, ref, irecv.at[6 + k]).wait()
         ref = col_ids.at[other[name]]
         pltpu.make_async_copy(ref, ref, irecv.at[14 + k]).wait()
+    id_cols = []
+    for k in range(8):
+        turned = jnp.transpose(jnp.broadcast_to(row_ids[k][:1], (128, 128)))
+        parts = [turned[at * 32 : (at + 1) * 32] for at in range(4)]
+        id_cols.append((parts[0] + parts[1]) + (parts[2] + parts[3]))
     for name in col_names:
         for q in range(4):
             cross_wait(name, q)
@@ -332,7 +351,7 @@
         )
         for k in range(8):
             part = products[k * 32 : (k + 1) * 32] * factor
-            same = jnp.concatenate([row_ids[k], row_ids[k]], axis=1) == ids
+            same = jnp.concatenate([id_cols[k], id_cols[k]], axis=1) == ids
             res_send[half, k] = jnp.where(same, 0.0, part).astype(BF)
         for k in (7, 3, 5, 6, 1, 2, 4):
             at = half * 7 + mirror[k] - 1
@@ -380,9 +399,8 @@
             pltpu.VMEM((16, 32, 4096), BF),
             pltpu.VMEM((2, 8, 32, 256), BF),
             pltpu.VMEM((2, 8, 32, 256), BF),
-            pltpu.VMEM((32, 128), jnp.int32),
             pltpu.VMEM((8, 128), jnp.int32),
-            pltpu.VMEM((8, 32, 128), jnp.int32),
+            pltpu.VMEM((8, 8, 128), jnp.int32),
             pltpu.VMEM((16, 8, 128), jnp.int32),
             pltpu.SemaphoreType.DMA((8,)),
             pltpu.SemaphoreType.DMA((6,)),

time: 43.3 us -> 42.3 us (0.977)
  Pallas kernels: 42.4 us -> 41.4 us
    pallas_call x1, Pallas kernels: 42.4 us -> 41.4 us  [on_device(): pl.pallas_call(functools.partial(kernel, factor=1.0 / (tokens * rank)), o...]
where the time goes in v4:
time: 42.3 us; the launch traced here: 42.2 us
  Pallas kernels  41.4 us (98%)
  local copies, waits for them, and re-layouts  0.8 us (2%)
    pallas_call x1, Pallas kernels, on_device(): pl.pallas_call(functools.partial(kernel, factor=1.0 / (tokens * rank)), o...  41.4 us

profile of v4, /device:TPU:1, one launch (start us, length us, event | category | flops | bytes accessed | tf_op | source)
XLA Modules:
  0.0 42.2 jit_solution(8213711528054858169)
XLA Ops:
  0.0 41.4 %influence.1 = f32[32,4096]{1,0:T(8,128)S(1)} custom-call(bf16[1024,4096]{1,0:T(8,128)(2,1)} %bitcast.4, bf16[1024,4096]{1,0:T(8,128)(2,1)} %bitcast.5, bf16[64,4096]{1,0:T(8,128)(2,1)} %bitcast.6, bf16[64,4096]{1,0:T(8,128)(2,1)} %bitcast.7, f32[64,64]{1,0:T(8,128)} %bin_hbm.1, f32[64,64]{1,0:T(8,128)} %bout_hbm.1, f32[64,64]{1,0:T(8,128)} %eig_hbm.1, ...), custom_call_target="tpu_custom_call" | custom-call | tf_op jit(solution)/shard_map/influence/pallas_call | solution.py:382
  41.4 0.8 %copy.10 = f32[32,4096]{1,0:T(8,128)} copy(f32[32,4096]{1,0:T(8,128)S(1)} %influence.1) | data formatting | bytes 1048576

commit v5 on v4

--- a/solution.py
+++ b/solution.py
@@ -329,26 +329,22 @@
         turned = jnp.transpose(jnp.broadcast_to(row_ids[k][:1], (128, 128)))
         parts = [turned[at * 32 : (at + 1) * 32] for at in range(4)]
         id_cols.append((parts[0] + parts[1]) + (parts[2] + parts[3]))
-    for name in col_names:
-        for q in range(4):
-            cross_wait(name, q)
 
     mine = x * 2 + lax.div(z, 2)
+    sides = (("own", "zc", "ym", "zcym"), ("yp", "zcyp", "y2", "zcy2"))
+    groups = ((y, ym), (yp, y2))
     for half in range(2):
-        block = pl.ds(half * 8, 8)
+        for name in sides[half]:
+            for q in range(4):
+                cross_wait(name, q)
+        blocks = [pl.ds(group * 4, 4) for group in groups[half]]
         products = lax.dot_general(
             rowbuf[...].reshape(256, 4096),
-            colbuf[block].reshape(256, 4096),
+            jnp.concatenate([colbuf[block].reshape(128, 4096) for block in blocks], axis=0),
             NT,
             preferred_element_type=F32,
         )
-        ids = jnp.concatenate(
-            [
-                jnp.sum(col_ids[pl.ds(half * 8 + 4 * part, 4)], axis=0)[:1]
-                for part in range(2)
-            ],
-            axis=1,
-        )
+        ids = jnp.concatenate([jnp.sum(col_ids[block], axis=0)[:1] for block in blocks], axis=1)
         for k in range(8):
             part = products[k * 32 : (k + 1) * 32] * factor
             same = jnp.concatenate([id_cols[k], id_cols[k]], axis=1) == ids
@@ -368,10 +364,10 @@
         for index in range(8):
             xi, k = index // 2, index % 2
             for side in range(2):
-                yi = half * 2 + side
-                at = (xi // 2) * 2048 + yi * 512 + (xi % 2) * 256 + k * 128
+                at = groups[half][side] * 512 + (xi // 2) * 2048 + (xi % 2) * 256 + k * 128
+                lanes = pl.ds(pl.multiple_of(at, 128), 128)
                 piece_of = res_recv[half, index, :, side * 128 : (side + 1) * 128]
-                out_ref[:, at : at + 128] = piece_of.astype(F32)
+                out_ref[:, lanes] = piece_of.astype(F32)
     for copy in started:
         copy.wait_send()
 

time: 42.3 us -> 41.3 us (0.976)
  Pallas kernels: 41.4 us -> 40.3 us
    pallas_call x1, Pallas kernels: 41.4 us -> 40.3 us  [on_device(): pl.pallas_call(functools.partial(kernel, factor=1.0 / (tokens * rank)), o...]
where the time goes in v5:
time: 41.3 us; the launch traced here: 41.1 us
  Pallas kernels  40.3 us (98%)
  local copies, waits for them, and re-layouts  0.8 us (2%)
    pallas_call x1, Pallas kernels, on_device(): pl.pallas_call(functools.partial(kernel, factor=1.0 / (tokens * rank)), o...  40.3 us

profile of v5, /device:TPU:1, one launch (start us, length us, event | category | flops | bytes accessed | tf_op | source)
XLA Modules:
  0.0 41.1 jit_solution(10607230934413478243)
XLA Ops:
  0.0 40.3 %influence.1 = f32[32,4096]{1,0:T(8,128)S(1)} custom-call(bf16[1024,4096]{1,0:T(8,128)(2,1)} %bitcast.4, bf16[1024,4096]{1,0:T(8,128)(2,1)} %bitcast.5, bf16[64,4096]{1,0:T(8,128)(2,1)} %bitcast.6, bf16[64,4096]{1,0:T(8,128)(2,1)} %bitcast.7, f32[64,64]{1,0:T(8,128)} %bin_hbm.1, f32[64,64]{1,0:T(8,128)} %bout_hbm.1, f32[64,64]{1,0:T(8,128)} %eig_hbm.1, ...), custom_call_target="tpu_custom_call" | custom-call | tf_op jit(solution)/shard_map/influence/pallas_call | solution.py:378
  40.3 0.8 %copy.10 = f32[32,4096]{1,0:T(8,128)} copy(f32[32,4096]{1,0:T(8,128)S(1)} %influence.1) | data formatting | bytes 1048576

commit v6 on v5

--- a/solution.py
+++ b/solution.py
@@ -299,9 +299,9 @@
     far_on(2)
     rest_on(0)
     rest_on(1)
+    z_on(2)
+    last_on(0)
     far_on(3)
-    last_on(0)
-    z_on(2)
     last_on(1)
     rest_on(2)
     z_on(3)

time: 41.3 us -> 41.3 us (level)
  no operation moved by 1% of the time
where the time goes in v6:
time: 41.3 us; the launch traced here: 41.1 us
  Pallas kernels  40.3 us (98%)
  local copies, waits for them, and re-layouts  0.8 us (2%)
    pallas_call x1, Pallas kernels, on_device(): pl.pallas_call(functools.partial(kernel, factor=1.0 / (tokens * rank)), o...  40.3 us

profile of v6, /device:TPU:1, one launch (start us, length us, event | category | flops | bytes accessed | tf_op | source)
XLA Modules:
  0.0 41.1 jit_solution(6555017345363357348)
XLA Ops:
  0.0 40.3 %influence.1 = f32[32,4096]{1,0:T(8,128)S(1)} custom-call(bf16[1024,4096]{1,0:T(8,128)(2,1)} %bitcast.4, bf16[1024,4096]{1,0:T(8,128)(2,1)} %bitcast.5, bf16[64,4096]{1,0:T(8,128)(2,1)} %bitcast.6, bf16[64,4096]{1,0:T(8,128)(2,1)} %bitcast.7, f32[64,64]{1,0:T(8,128)} %bin_hbm.1, f32[64,64]{1,0:T(8,128)} %bout_hbm.1, f32[64,64]{1,0:T(8,128)} %eig_hbm.1, ...), custom_call_target="tpu_custom_call" | custom-call | tf_op jit(solution)/shard_map/influence/pallas_call | solution.py:378
  40.3 0.8 %copy.10 = f32[32,4096]{1,0:T(8,128)} copy(f32[32,4096]{1,0:T(8,128)S(1)} %influence.1) | data formatting | bytes 1048576
